TPU v7x, 32 devices: a whole 2x2x4 slice. The times are simulated.
32 devices in a mesh: rows: 16 (over z, x, core), cols: 2 (over y).
Axes of the slice: x: 2, y: 2, z: 4, core: 2. Of those that a mesh axis runs over, the one named last changes fastest.
Arguments:
- unfolding: float32 [8192, 4096], P('rows', 'cols'), may hold values from -6 to 6
- pattern: int32 [32, 2], P('cols'), may hold values from 0 to 1, as said below
- sign_bits: int32 [4096, 2], P('cols'), may hold values from 0 to 1
Outputs:
- core_scaled: float32 [8192, 256], P('rows')
- next_unfolding: float32 [2048, 512], P('rows', 'cols')
Inputs may be any that keep to these rules, and one draw needn't show every extreme that they name: Every row and every column of pattern holds at least one 1, and some entry is 0.
All inputs are finite; a program needn't handle non-finite values.
Results may differ from a plain program's by a relative error of at most 0.00017.
Values sent between devices are 32-bit elements; how exact they have to be, the bound alone decides.
No kernel may reach another device: no remote copies, remote signals or barrier semaphores. Data moves between devices by JAX's collectives and lax.ppermute only.
A program may use at most 64 MiB of HBM per device.

v0:
```python
import math
import jax
import jax.numpy as jnp
from jax import lax
from jax.sharding import PartitionSpec as P

RANK = 256
BLK = 128
MODE = 8


def hadamard_table(table_size):
    row_index = lax.broadcasted_iota(jnp.int32, (table_size, table_size), 0)
    col_index = lax.broadcasted_iota(jnp.int32, (table_size, table_size), 1)
    parity = jnp.zeros((table_size, table_size), jnp.int32)
    for bit_level in range(table_size.bit_length() - 1):
        bit_value = 1 << bit_level
        parity = parity + row_index // bit_value % 2 * (col_index // bit_value % 2)
    return (1 - 2 * (parity % 2)).astype(jnp.float32)


def sketch_matrix(pattern, sign_bits, block_size):
    blocks = sign_bits.shape[1]
    rows_here = sign_bits.shape[0]
    hadamard = hadamard_table(block_size)
    factor = jnp.repeat(pattern, block_size, axis=0) * (2 * sign_bits - 1)
    tiled_table = jnp.tile(hadamard, (rows_here // block_size, 1))
    expanded = factor.astype(jnp.float32)[:, :, None] * tiled_table[:, None, :]
    return expanded.reshape(rows_here, blocks * block_size)


def inner_rows(left_side, right_side):
    return lax.dot_general(
        left_side, right_side, (((0,), (0,)), ((), ())), precision=lax.Precision.HIGHEST
    )


def local(unfolding, pattern, sign_bits):
    highest = lax.Precision.HIGHEST
    sketch_map = sketch_matrix(pattern, sign_bits, BLK)
    local_rows = unfolding.shape[0]
    local_cols = unfolding.shape[1]
    row_devices = lax.axis_size("rows")
    col_devices = lax.axis_size("cols")
    total_rows = local_rows * row_devices
    partial_sketch = jnp.dot(unfolding, sketch_map, precision=highest)
    sketch = lax.psum(partial_sketch, "cols")
    gram_matrix = lax.psum(inner_rows(sketch, sketch), "rows")
    gram_matrix = gram_matrix + float(total_rows) * jnp.eye(RANK, dtype=jnp.float32)
    lower_factor = jnp.linalg.cholesky(gram_matrix)
    basis_rows = lax.linalg.triangular_solve(
        lower_factor, sketch, left_side=False, lower=True, transpose_a=True
    )
    core_scaled = basis_rows * math.sqrt(total_rows)
    mode_local = MODE // col_devices
    rest_cols = local_cols // mode_local
    rank_share = RANK // row_devices
    reduced = lax.psum_scatter(
        inner_rows(basis_rows, unfolding), "rows", scatter_dimension=0, tiled=True
    )
    grouped = reduced.reshape(rank_share, mode_local, rest_cols)
    regrouped = lax.all_to_all(grouped, "cols", split_axis=2, concat_axis=1, tiled=True)
    next_unfolding = regrouped.reshape(rank_share * MODE, regrouped.shape[2])
    return (core_scaled, next_unfolding)


def solution(mesh):
    in_specs = (P("rows", "cols"), P("cols", None), P("cols", None))
    out_specs = (P("rows", None), P("rows", "cols"))
    return jax.shard_map(local, mesh=mesh, in_specs=in_specs, out_specs=out_specs, check_vma=False)
```

profile of v0, /device:TPU:0, one launch (start us, length us, event | category | flops | bytes accessed | tf_op | source)
XLA Modules:
  0.0 304.2 jit_solution(9669718208111324517)
XLA Ops:
  7.2 0.0 copy-start
  7.2 0.0 all-reduce.4.cloned.1.call-start
  7.3 0.5 copy-done
  7.8 0.1 broadcast_bitcast_fusion
  7.9 0.7 fusion.51
  8.7 0.4 copy.24
  9.0 0.4 fusion.27
  9.4 0.1 tile.8
  9.5 0.0 copy-start.1
  9.5 7.7 %broadcast_multiply_fusion = f32[2048,2,128]{2,1,0:T(2,128)S(1)} fusion(f32[2048,128]{1,0:T(8,128)S(1)} %bitcast.58, f32[2048,2]{1,0:T(8,128)S(1)} %copy.24), kind=kLoop, calls=%fused_computation.8 | loop fusion | flops 524288 | bytes 3162112 | tf_op jit(solution)/shard_map/mul | solution.py:28
  17.3 0.0 copy-done.1
  17.3 8.1 %fusion.3 = f32[512,256]{0,1:T(8,128)} fusion(f32[512,2048]{1,0:T(8,128)S(1)} %copy-done.1, f32[256,8,2,128]{3,2,1,0:T(2,128)S(1)} %bitcast.55), kind=kOutput, calls=%fused_computation.5 | convolution fusion | flops 3221225472 | bytes 6815744 | tf_op jit(solution)/shard_map/dot_general | solution.py:46
  25.4 0.0 all-reduce.4.cloned.1.call-update
  25.4 0.0 all-reduce.6.cloned.1.call-start
  25.5 31.4 %all-reduce.4.cloned.1.call-done = f32[512,256]{0,1:T(8,128)} async-done(((f32[512,256]{0,1:T(8,128)}), f32[512,256]{0,1:T(8,128)}) %all-reduce.4.cloned.1.call-update) | async-done | bytes 524304 | tf_op jit(solution)/shard_map/psum | solution.py:47
  56.9 2.5 fusion.55
  59.4 0.0 all-reduce.6.cloned.1.call-update
  59.4 0.2 reduce-scatter.2.cloned.1.call-start
  59.7 90.3 %all-reduce.6.cloned.1.call-done = f32[256,256]{0,1:T(8,128)} async-done(((f32[256,256]{0,1:T(8,128)}), f32[256,256]{0,1:T(8,128)}) %all-reduce.6.cloned.1.call-update) | async-done | bytes 262160 | tf_op jit(solution)/shard_map/psum | solution.py:48
  150.0 1.0 select_add_fusion
  150.9 0.1 copy.26
  151.1 1.0 fusion.10
  152.1 11.7 %cholesky.45 = f32[128,128]{1,0:T(8,128)S(1)} custom-call(f32[128,128]{1,0:T(8,128)S(1)} %cholesky.107), custom_call_target="Cholesky" | custom-call | tf_op jit(solution)/shard_map/jit(cholesky)/cholesky | solution.py:50
  163.8 0.0 copy-start.2
  163.8 9.8 %custom-call.14 = f32[1,128,128]{1,2,0:T(8,128)S(1)} custom-call(f32[1,128,128]{2,1,0:T(8,128)S(1)} %get-tuple-element.39), custom_call_target="InvertDiagBlocksLowerTriangular" | custom-call | tf_op jit(solution)/shard_map/jit(cholesky)/cholesky | solution.py:50
  173.7 0.2 fusion.42
  173.9 0.3 convolution_subtract_fusion.1
  174.1 11.7 %cholesky.95 = f32[128,128]{1,0:T(8,128)S(1)} custom-call(f32[128,128]{1,0:T(8,128)S(1)} %convolution_subtract_fusion.1), custom_call_target="Cholesky" | custom-call | tf_op jit(solution)/shard_map/jit(cholesky)/cholesky | solution.py:50
  185.9 0.1 copy.29
  186.0 0.1 copy.28
  186.1 0.1 copy.27
  186.2 0.7 compare_reduce_fusion
  186.9 0.6 compare_reduce_fusion.1
  188.9 0.1 triangular_solve.61
  188.9 4.3 %while.1 = (s32[]{:T(128)}, f32[256,256]{0,1:T(8,128)S(1)}, s32[2,2]{1,0:T(2,128)S(1)}, f32[2,128,128]{2,1,0:T(8,128)S(1)}, s32[]{:T(128)}) while((s32[]{:T(128)}, f32[256,256]{0,1:T(8,128)S(1)}, s32[2,2]{1,0:T(2,128)S(1)}, f32[2,128,128]{2,1,0:T(8,128)S(1)}, s32[]{:T(128)}) %tuple.39), condition=%wide.while_cond, body=%wide.while_body.sunk | while | flops 2 | bytes 393321 | solution.py:51
  189.1 0.6 fusion.65
  189.7 1.3 dynamic-slice.7
  191.0 0.1 copy.48
  191.2 0.6 fusion.65
  191.8 1.3 dynamic-slice.7
  193.1 0.1 copy.48
  193.3 19.7 %custom-call.15 = f32[2,128,128]{1,2,0:T(8,128)S(1)} custom-call(f32[2,128,128]{2,1,0:T(8,128)S(1)} %get-tuple-element.9), custom_call_target="InvertDiagBlocksLowerTriangular" | custom-call | tf_op jit(solution)/shard_map/triangular_solve | solution.py:51
  212.9 0.0 copy-done.2
  212.9 0.4 fusion.8
  213.4 0.4 convolution_subtract_fusion
  213.8 0.4 fusion.40
  214.2 7.2 %fusion.6 = f32[256,2048]{1,0:T(8,128)} fusion(f32[512,2048]{1,0:T(8,128)} %param.3, f32[512,128]{0,1:T(8,128)S(1)} %fusion.40, f32[512,128]{0,1:T(8,128)S(1)} %fusion.8), kind=kOutput, calls=%fused_computation.10 | convolution fusion | flops 3221356544 | bytes 6815744 | tf_op jit(solution)/shard_map/dot_general | solution.py:33
  221.4 0.0 reduce-scatter.2.cloned.1.call-update
  221.4 62.2 %reduce-scatter.2.cloned.1.call-done = f32[16,2048]{1,0:T(8,128)} async-done(((f32[256,2048]{1,0:T(8,128)}), f32[16,2048]{1,0:T(8,128)}) %reduce-scatter.2.cloned.1.call-update) | async-done | bytes 131088 | tf_op jit(solution)/shard_map/reduce_scatter | solution.py:58
  283.6 1.0 reshape.692
  284.6 0.4 copy.32
  285.0 1.5 reshape.713
  286.5 3.4 %all-to-all-start = ((f32[2,1,16384]{2,1,0:T(1,128)}), f32[2,1,16384]{2,1,0:T(1,128)S(1)}, u32[]{:S(2)}, u32[]{:S(2)}) async-start(f32[2,1,16384]{2,1,0:T(1,128)} %reshape.713), calls=%async_computation.1 | async-start | bytes 262144 | tf_op jit(solution)/shard_map/all_to_all | solution.py:62
  289.9 0.1 fusion.7
  289.9 1.0 copy.34
  290.9 3.4 %all-to-all-done = f32[2,1,16384]{2,1,0:T(1,128)S(1)} async-done(((f32[2,1,16384]{2,1,0:T(1,128)}), f32[2,1,16384]{2,1,0:T(1,128)S(1)}, u32[]{:S(2)}, u32[]{:S(2)}) %all-to-all-start) | async-done | bytes 131104 | tf_op jit(solution)/shard_map/all_to_all | solution.py:62
  294.3 0.5 broadcast.1149
  294.8 1.0 reduce.12
  295.9 0.8 reshape.714
  296.6 0.3 copy.33
  297.0 0.7 reshape.693
  (22 shorter events, 0.2 us)
Async XLA Ops:
  7.2 0.7 copy-start
  7.2 49.7 %all-reduce.4.cloned.1.call-start = ((), (), s32[]{:S(2)}) async-start(), calls=%async_computation.2 | async-start | bytes 1048576 | tf_op jit(solution)/shard_map/psum | solution.py:47
  9.5 7.8 %copy-start.1 = (f32[512,2048]{1,0:T(8,128)S(1)}, f32[512,2048]{1,0:T(8,128)}, u32[]{:S(2)}) copy-start(f32[512,2048]{1,0:T(8,128)} %param.3) | copy-start | bytes 12582916
  25.4 124.6 %all-reduce.6.cloned.1.call-start = ((), (), s32[]{:S(2)}) async-start(), calls=%async_computation.3 | async-start | bytes 524288 | tf_op jit(solution)/shard_map/psum | solution.py:48
  59.4 224.2 %reduce-scatter.2.cloned.1.call-start = ((), (), s32[]{:S(2)}) async-start(), calls=%async_computation.4 | async-start | bytes 2228224 | tf_op jit(solution)/shard_map/reduce_scatter | solution.py:58
  163.8 49.1 %copy-start.2 = (f32[512,256]{0,1:T(8,128)S(1)}, f32[512,256]{0,1:T(8,128)}, u32[]{:S(2)}) copy-start(f32[512,256]{0,1:T(8,128)} %all-reduce.4.cloned.1.call-done) | copy-start | bytes 1572868
  286.5 7.8 %all-to-all-start = ((f32[2,1,16384]{2,1,0:T(1,128)}), f32[2,1,16384]{2,1,0:T(1,128)S(1)}, u32[]{:S(2)}, u32[]{:S(2)}) async-start(f32[2,1,16384]{2,1,0:T(1,128)} %reshape.713), calls=%async_computation.1 | async-start | bytes 262144 | tf_op jit(solution)/shard_map/all_to_all | solution.py:62
Sparse Core Ops, SparseCore 0:
  25.5 31.2 all-reduce.3
  61.2 88.7 all-reduce.5
  221.5 62.0 reduce-scatter.1
where the time goes:
time: 305 us; the launch traced here: 304 us
  waiting for transfers between devices  187 us (61%)
  other arithmetic  66.3 us (22%)
  matrix products  19.5 us (6%)
  between operations  15.3 us (5%)
  local copies, waits for them, and re-layouts  11.8 us (4%)
  starting transfers between devices  3.68 us (1%)
    psum x1, waiting for transfers between devices, local(): gram_matrix = lax.psum(inner_rows(sketch, sketch), 'rows')  90.3 us
    reduce_scatter x1, waiting for transfers between devices, local(): lax.psum_scatter(inner_rows(basis_rows, unfolding), 'rows', scatter_dimen...  62.2 us
    another operation x7, other arithmetic, local(): lower_factor = jnp.linalg.cholesky(gram_matrix)  34.6 us
    psum x1, waiting for transfers between devices, local(): sketch = lax.psum(partial_sketch, 'cols')  31.4 us
    another operation x3, other arithmetic, local(): lax.linalg.triangular_solve(lower_factor, sketch, left_side=False, lower=...  19.7 us
    dot_general x2, matrix products, inner_rows(): lax.dot_general(left_side, right_side, (((0,), (0,)), ((), ())), precisio...  9.68 us
    dot_general x1, matrix products, local(): partial_sketch = jnp.dot(unfolding, sketch_map, precision=highest)  8.08 us
    mul x1, other arithmetic, sketch_matrix(): expanded = factor.astype(jnp.float32)[:, :, None] * tiled_table[:, None, :]  7.74 us
  transfers between devices with their start and end apart: 4, of which 4 were waited for; matrix products, arithmetic and copies ran while one was open for 0% of the time, Pallas kernels for 0%

commit v1 on v0

--- a/solution.py
+++ b/solution.py
@@ -45,7 +45,7 @@
     total_rows = local_rows * row_devices
     partial_sketch = jnp.dot(unfolding, sketch_map, precision=highest)
     sketch = lax.psum(partial_sketch, "cols")
-    gram_matrix = lax.psum(inner_rows(sketch, sketch), "rows")
+    gram_matrix = jnp.sum(lax.all_gather(inner_rows(sketch, sketch), "rows"), axis=0)
     gram_matrix = gram_matrix + float(total_rows) * jnp.eye(RANK, dtype=jnp.float32)
     lower_factor = jnp.linalg.cholesky(gram_matrix)
     basis_rows = lax.linalg.triangular_solve(

time: 305 us -> 263 us (0.86)
  waiting for transfers between devices: 187 us -> 146 us
    psum x1 -> x0, waiting for transfers between devices: 90.3 us -> none  [local(): gram_matrix = lax.psum(inner_rows(sketch, sketch), 'rows')]
    all_gather x0 -> x1, waiting for transfers between devices: none -> 50.9 us  [local(): lax.all_gather(inner_rows(sketch, sketch), 'rows')]
where the time goes in v1:
time: 263 us
  waiting for transfers between devices  146 us (56%)
  other arithmetic  66.8 us (25%)
  matrix products  19.4 us (7%)
  between operations  15.3 us (6%)
  local copies, waits for them, and re-layouts  11.4 us (4%)
  starting transfers between devices  3.68 us (1%)
    reduce_scatter x1, waiting for transfers between devices, local(): lax.psum_scatter(inner_rows(basis_rows, unfolding), 'rows', scatter_dimen...  60.2 us
    all_gather x1, waiting for transfers between devices, local(): lax.all_gather(inner_rows(sketch, sketch), 'rows')  50.9 us
    another operation x7, other arithmetic, local(): lower_factor = jnp.linalg.cholesky(gram_matrix)  34.6 us
    psum x1, waiting for transfers between devices, local(): sketch = lax.psum(partial_sketch, 'cols')  31.4 us
    another operation x3, other arithmetic, local(): lax.linalg.triangular_solve(lower_factor, sketch, left_side=False, lower=...  19.7 us
    dot_general x2, matrix products, inner_rows(): lax.dot_general(left_side, right_side, (((0,), (0,)), ((), ())), precisio...  9.67 us
    dot_general x1, matrix products, local(): partial_sketch = jnp.dot(unfolding, sketch_map, precision=highest)  8.08 us
    mul x1, other arithmetic, sketch_matrix(): expanded = factor.astype(jnp.float32)[:, :, None] * tiled_table[:, None, :]  7.74 us
  transfers between devices with their start and end apart: 4, of which 4 were waited for; matrix products, arithmetic and copies ran while one was open for 0% of the time, Pallas kernels for 0%

profile of v1, /device:TPU:0, one launch (start us, length us, event | category | flops | bytes accessed | tf_op | source)
XLA Modules:
  0.0 262.8 jit_solution(6539153903838008490)
XLA Ops:
  7.2 0.0 copy-start
  7.2 0.0 all-reduce.3.cloned.1.call-start
  7.3 0.5 copy-done
  7.8 0.1 broadcast_bitcast_fusion
  7.9 0.7 fusion.50
  8.7 0.4 copy.14
  9.0 0.4 fusion.26
  9.4 0.1 tile.8
  9.5 0.0 copy-start.1
  9.5 7.7 %broadcast_multiply_fusion = f32[2048,2,128]{2,1,0:T(2,128)S(1)} fusion(f32[2048,128]{1,0:T(8,128)S(1)} %bitcast.59, f32[2048,2]{1,0:T(8,128)S(1)} %copy.14), kind=kLoop, calls=%fused_computation.8 | loop fusion | flops 524288 | bytes 3162112 | tf_op jit(solution)/shard_map/mul | solution.py:28
  17.3 0.0 copy-done.1
  17.3 8.1 %fusion.3 = f32[512,256]{0,1:T(8,128)} fusion(f32[512,2048]{1,0:T(8,128)S(1)} %copy-done.1, f32[256,8,2,128]{3,2,1,0:T(2,128)S(1)} %bitcast.55), kind=kOutput, calls=%fused_computation.5 | convolution fusion | flops 3221225472 | bytes 6815744 | tf_op jit(solution)/shard_map/dot_general | solution.py:46
  25.4 0.0 all-reduce.3.cloned.1.call-update
  25.4 0.0 all-gather.3.cloned.1.call-start
  25.5 31.4 %all-reduce.3.cloned.1.call-done = f32[512,256]{0,1:T(8,128)} async-done(((f32[512,256]{0,1:T(8,128)}), f32[512,256]{0,1:T(8,128)}) %all-reduce.3.cloned.1.call-update) | async-done | bytes 524304 | tf_op jit(solution)/shard_map/psum | solution.py:47
  56.9 2.5 fusion.54
  59.4 0.0 all-gather.3.cloned.1.call-update
  59.4 0.2 reduce-scatter.2.cloned.1.call-start
  59.7 50.9 %all-gather.3.cloned.1.call-done = f32[4096,256]{1,0:T(8,128)} async-done(((f32[256,256]{1,0:T(8,128)}), f32[4096,256]{1,0:T(8,128)}) %all-gather.3.cloned.1.call-update) | async-done | bytes 4194320 | tf_op jit(solution)/shard_map/all_gather | solution.py:48
  110.6 2.5 reduce_sum.11
  113.1 0.0 copy-start.2
  113.1 0.1 copy.15
  113.2 0.1 add_multiply_fusion
  113.3 11.7 %cholesky.45 = f32[128,128]{1,0:T(8,128)S(1)} custom-call(f32[128,128]{1,0:T(8,128)S(1)} %cholesky.107), custom_call_target="Cholesky" | custom-call | tf_op jit(solution)/shard_map/jit(cholesky)/cholesky | solution.py:50
  125.1 9.8 %custom-call.14 = f32[1,128,128]{1,2,0:T(8,128)S(1)} custom-call(f32[1,128,128]{2,1,0:T(8,128)S(1)} %get-tuple-element.29), custom_call_target="InvertDiagBlocksLowerTriangular" | custom-call | tf_op jit(solution)/shard_map/jit(cholesky)/cholesky | solution.py:50
  134.9 0.2 constant_dynamic-update-slice_fusion.1
  135.1 0.3 convolution_subtract_fusion.1
  135.3 11.7 %cholesky.95 = f32[128,128]{1,0:T(8,128)S(1)} custom-call(f32[128,128]{1,0:T(8,128)S(1)} %convolution_subtract_fusion.1), custom_call_target="Cholesky" | custom-call | tf_op jit(solution)/shard_map/jit(cholesky)/cholesky | solution.py:50
  147.1 0.7 compare_reduce_fusion
  147.7 0.6 compare_reduce_fusion.1
  149.7 0.1 triangular_solve.64
  149.8 4.1 %while.1 = (s32[]{:T(128)}, f32[256,256]{1,0:T(8,128)S(1)}, s32[2,2]{1,0:T(2,128)S(1)}, f32[2,128,128]{2,1,0:T(8,128)S(1)}, s32[]{:T(128)}) while((s32[]{:T(128)}, f32[256,256]{1,0:T(8,128)S(1)}, s32[2,2]{1,0:T(2,128)S(1)}, f32[2,128,128]{2,1,0:T(8,128)S(1)}, s32[]{:T(128)}) %tuple.38), condition=%wide.while_cond, body=%wide.while_body.sunk | while | flops 2 | bytes 131181 | solution.py:51
  149.9 0.6 fusion.64
  150.5 1.4 bitcast_dynamic-update-slice_fusion.2
  151.9 0.6 fusion.64
  152.5 1.4 bitcast_dynamic-update-slice_fusion.2
  153.9 19.7 %custom-call.15 = f32[2,128,128]{1,2,0:T(8,128)S(1)} custom-call(f32[2,128,128]{2,1,0:T(8,128)S(1)} %get-tuple-element.9), custom_call_target="InvertDiagBlocksLowerTriangular" | custom-call | tf_op jit(solution)/shard_map/triangular_solve | solution.py:51
  173.6 0.0 copy-done.2
  173.6 0.4 fusion.8
  174.0 0.4 convolution_subtract_fusion
  174.4 0.4 fusion.39
  174.8 7.1 %fusion.6 = f32[256,2048]{1,0:T(8,128)} fusion(f32[512,2048]{1,0:T(8,128)} %param.3, f32[512,128]{0,1:T(8,128)S(1)} %fusion.39, f32[512,128]{0,1:T(8,128)S(1)} %fusion.8), kind=kOutput, calls=%fused_computation.10 | convolution fusion | flops 3221356544 | bytes 6815744 | tf_op jit(solution)/shard_map/dot_general | solution.py:33
  182.0 0.0 reduce-scatter.2.cloned.1.call-update
  182.0 60.2 %reduce-scatter.2.cloned.1.call-done = f32[16,2048]{1,0:T(8,128)} async-done(((f32[256,2048]{1,0:T(8,128)}), f32[16,2048]{1,0:T(8,128)}) %reduce-scatter.2.cloned.1.call-update) | async-done | bytes 131088 | tf_op jit(solution)/shard_map/reduce_scatter | solution.py:58
  242.2 1.0 reshape.692
  243.2 0.4 copy.17
  243.6 1.5 reshape.714
  245.1 3.4 %all-to-all-start = ((f32[2,1,16384]{2,1,0:T(1,128)}), f32[2,1,16384]{2,1,0:T(1,128)S(1)}, u32[]{:S(2)}, u32[]{:S(2)}) async-start(f32[2,1,16384]{2,1,0:T(1,128)} %reshape.714), calls=%async_computation.1 | async-start | bytes 262144 | tf_op jit(solution)/shard_map/all_to_all | solution.py:62
  248.5 0.1 fusion.7
  248.5 1.0 copy.19
  249.5 3.4 %all-to-all-done = f32[2,1,16384]{2,1,0:T(1,128)S(1)} async-done(((f32[2,1,16384]{2,1,0:T(1,128)}), f32[2,1,16384]{2,1,0:T(1,128)S(1)}, u32[]{:S(2)}, u32[]{:S(2)}) %all-to-all-start) | async-done | bytes 131104 | tf_op jit(solution)/shard_map/all_to_all | solution.py:62
  252.9 0.5 broadcast.1149
  253.4 1.0 reduce.12
  254.4 0.8 reshape.715
  255.2 0.3 copy.18
  255.5 0.7 reshape.693
  (18 shorter events, 0.2 us)
Async XLA Ops:
  7.2 0.7 copy-start
  7.2 49.7 %all-reduce.3.cloned.1.call-start = ((), (), s32[]{:S(2)}) async-start(), calls=%async_computation.2 | async-start | bytes 1048576 | tf_op jit(solution)/shard_map/psum | solution.py:47
  9.5 7.8 %copy-start.1 = (f32[512,2048]{1,0:T(8,128)S(1)}, f32[512,2048]{1,0:T(8,128)}, u32[]{:S(2)}) copy-start(f32[512,2048]{1,0:T(8,128)} %param.3) | copy-start | bytes 12582916
  25.4 85.2 %all-gather.3.cloned.1.call-start = ((), (), s32[]{:S(2)}) async-start(), calls=%async_computation.4 | async-start | bytes 4456448 | tf_op jit(solution)/shard_map/all_gather | solution.py:48
  59.4 182.8 %reduce-scatter.2.cloned.1.call-start = ((), (), s32[]{:S(2)}) async-start(), calls=%async_computation.3 | async-start | bytes 2228224 | tf_op jit(solution)/shard_map/reduce_scatter | solution.py:58
  113.1 60.5 %copy-start.2 = (f32[512,256]{0,1:T(8,128)S(1)}, f32[512,256]{0,1:T(8,128)}, u32[]{:S(2)}) copy-start(f32[512,256]{0,1:T(8,128)} %all-reduce.3.cloned.1.call-done) | copy-start | bytes 1572868
  245.1 7.8 %all-to-all-start = ((f32[2,1,16384]{2,1,0:T(1,128)}), f32[2,1,16384]{2,1,0:T(1,128)S(1)}, u32[]{:S(2)}, u32[]{:S(2)}) async-start(f32[2,1,16384]{2,1,0:T(1,128)} %reshape.714), calls=%async_computation.1 | async-start | bytes 262144 | tf_op jit(solution)/shard_map/all_to_all | solution.py:62
Sparse Core Ops, SparseCore 0:
  25.5 31.2 all-reduce.2
  59.8 50.7 all-gather.2
  182.1 60.0 reduce-scatter.1
